TPU v7x, 32 devices: a whole 2x2x4 slice. The times are simulated.
32 devices in a mesh: fsdp: 8 (over z, x), tp: 4 (over y, core).
Axes of the slice: x: 2, y: 2, z: 4, core: 2. Of those that a mesh axis runs over, the one named last changes fastest.
Arguments:
- tokens: bfloat16 [1024, 4096], P('fsdp'), may hold values from -6 to 6
- gate_left: bfloat16 [4096, 1024], P('fsdp', 'tp'), may hold values from -0.09375 to 0.09375
- gate_right: bfloat16 [1024, 14336], P('fsdp', 'tp'), may hold values from -0.1875 to 0.1875
- gate_values: bfloat16 [108, 16384], P('tp', 'fsdp'), may hold values from -0.5 to 0.5
- gate_rows: int32 [108], P('tp'), may hold values from 0 to 31
- gate_cols: int32 [108], P('tp'), may hold values from 0 to 111, as said below
- up_left: bfloat16 [4096, 1024], P('fsdp', 'tp'), may hold values from -0.09375 to 0.09375
- up_right: bfloat16 [1024, 14336], P('fsdp', 'tp'), may hold values from -0.1875 to 0.1875
- up_values: bfloat16 [108, 16384], P('tp', 'fsdp'), may hold values from -0.5 to 0.5
- up_rows: int32 [108], P('tp'), may hold values from 0 to 31
- up_cols: int32 [108], P('tp'), may hold values from 0 to 111, as said below
- grad_hidden: bfloat16 [1024, 14336], P('fsdp', 'tp'), may hold values from -6 to 6
Outputs:
- hidden: bfloat16 [1024, 14336], P('fsdp', 'tp')
- grad_gate_values: float32 [108, 16384], P('tp', 'fsdp')
- grad_up_values: float32 [108, 16384], P('tp', 'fsdp')
Inputs may be any that keep to these rules, and one draw needn't show every extreme that they name: `gate_cols`: support blocks of one projection are distinct (row block, column block) pairs; the entries that lie on index t of tp have column blocks from t * 14336 // (128 * 4) to (t + 1) * 14336 // (128 * 4) - 1. Rows and columns of one projection go together. `up_cols`: as for the gate projection.
All inputs are finite; a program needn't handle non-finite values.
Results may differ from a plain program's by a relative error of at most 0.005.
Values may be sent and summed in bfloat16 or wider, within the bound.
No kernel may reach another device: no remote copies, remote signals or barrier semaphores. Data moves between devices by JAX's collectives and lax.ppermute only.
A program may use at most 128 MiB of HBM per device.

v0:
```python
import jax
import jax.numpy as jnp
from jax import lax
from jax.sharding import PartitionSpec as P

BLK = 128


def support_forward(tokens, blocks, rows, cols_local, col_blocks):
    width = tokens.shape[1] // BLK
    sources = tokens.reshape(tokens.shape[0], width, BLK)[:, rows, :]
    parts = jnp.einsum("tkb,kbc->tkc", sources, blocks, preferred_element_type=jnp.float32)
    placed = (
        jnp.zeros((tokens.shape[0], col_blocks, BLK), jnp.float32).at[:, cols_local, :].add(parts)
    )
    return (placed.reshape(tokens.shape[0], col_blocks * BLK), sources)


def value_terms(sources_gate, dpre_gate, local_gate, sources_up, dpre_up, local_up, col_blocks):
    picked_gate = dpre_gate.reshape(dpre_gate.shape[0], col_blocks, BLK)[:, local_gate, :]
    picked_up = dpre_up.reshape(dpre_up.shape[0], col_blocks, BLK)[:, local_up, :]
    value_gate = jnp.einsum(
        "tkb,tkc->kbc", sources_gate, picked_gate, preferred_element_type=jnp.float32
    )
    value_up = jnp.einsum("tkb,tkc->kbc", sources_up, picked_up, preferred_element_type=jnp.float32)
    return (
        value_gate.reshape(value_gate.shape[0], BLK * BLK),
        value_up.reshape(value_up.shape[0], BLK * BLK),
    )


def on_device(
    tokens,
    gate_left,
    gate_right,
    gate_values,
    gate_rows,
    gate_cols,
    up_left,
    up_right,
    up_values,
    up_rows,
    up_cols,
    grad_hidden,
):
    left_gate, left_up = (
        lax.all_gather(gate_left, "fsdp", axis=0, tiled=True),
        lax.all_gather(up_left, "fsdp", axis=0, tiled=True),
    )
    rank_gate = jnp.dot(tokens, left_gate, preferred_element_type=jnp.float32).astype(jnp.bfloat16)
    rank_up = jnp.dot(tokens, left_up, preferred_element_type=jnp.float32).astype(jnp.bfloat16)
    full_gate, full_up = (
        lax.all_gather(rank_gate, "tp", axis=1, tiled=True),
        lax.all_gather(rank_up, "tp", axis=1, tiled=True),
    )
    flat_gate, flat_up = (
        lax.all_gather(gate_values, "fsdp", axis=1, tiled=True),
        lax.all_gather(up_values, "fsdp", axis=1, tiled=True),
    )
    blocks_gate = flat_gate.reshape(flat_gate.shape[0], BLK, BLK)
    blocks_up = flat_up.reshape(flat_up.shape[0], BLK, BLK)
    right_gate = lax.all_gather(gate_right, "fsdp", axis=0, tiled=True)
    right_up = lax.all_gather(up_right, "fsdp", axis=0, tiled=True)
    col_blocks = right_gate.shape[1] // BLK
    col_base = lax.axis_index("tp") * col_blocks
    local_gate = gate_cols - col_base
    local_up = up_cols - col_base
    sparse_gate, sources_gate = support_forward(
        tokens, blocks_gate, gate_rows, local_gate, col_blocks
    )
    sparse_up, sources_up = support_forward(tokens, blocks_up, up_rows, local_up, col_blocks)
    pre_gate = jnp.dot(full_gate, right_gate, preferred_element_type=jnp.float32) + sparse_gate
    pre_up = jnp.dot(full_up, right_up, preferred_element_type=jnp.float32) + sparse_up
    sigma = jax.nn.sigmoid(pre_gate)
    silu = pre_gate * sigma
    upstream = grad_hidden.astype(jnp.float32)
    dpre_gate = (upstream * pre_up * sigma * (1.0 + pre_gate * (1.0 - sigma))).astype(jnp.bfloat16)
    dpre_up = (upstream * silu).astype(jnp.bfloat16)
    hidden = (silu * pre_up).astype(jnp.bfloat16)
    value_gate, value_up = value_terms(
        sources_gate, dpre_gate, local_gate, sources_up, dpre_up, local_up, col_blocks
    )
    grad_gate_values, grad_up_values = (
        lax.psum_scatter(value_gate, "fsdp", scatter_dimension=1, tiled=True),
        lax.psum_scatter(value_up, "fsdp", scatter_dimension=1, tiled=True),
    )
    return (hidden, grad_gate_values, grad_up_values)


def solution(mesh):
    return jax.shard_map(
        on_device,
        mesh=mesh,
        in_specs=(
            P("fsdp", None),
            P("fsdp", "tp"),
            P("fsdp", "tp"),
            P("tp", "fsdp"),
            P("tp"),
            P("tp"),
            P("fsdp", "tp"),
            P("fsdp", "tp"),
            P("tp", "fsdp"),
            P("tp"),
            P("tp"),
            P("fsdp", "tp"),
        ),
        out_specs=(P("fsdp", "tp"), P("tp", "fsdp"), P("tp", "fsdp")),
        check_vma=False,
    )
```

profile of v0, /device:TPU:0, one launch (start us, length us, event | category | flops | bytes accessed | tf_op | source)
XLA Modules:
  0.0 506.7 jit_solution(9324583249922640998)
XLA Ops:
  7.2 0.7 all-gather.5.cloned.1.call-update
  8.0 0.7 all-gather.9.cloned.1.call-update
  8.7 0.7 all-gather.7.cloned.1.call-update
  9.4 0.5 all-gather.11.cloned.1.call-update
  10.0 0.7 copy.29
  10.7 0.7 copy.30
  11.4 36.4 %all_gather.27 = bf16[27,16384]{1,0:T(8,128)(2,1)S(1)} all-gather(bf16[27,2048]{1,0:T(8,128)(2,1)S(1)} %copy-done.9), channel_id=1, replica_groups=mesh['fsdp'=8,'tp'=4] {'fsdp'}, dimensions={1}, use_global_device_ids=true | all-gather | bytes 995328 | tf_op jit(solution)/shard_map/all_gather | solution.py:57
  47.8 1.2 copy.44
  49.0 0.7 gather_fusion
  49.8 3.1 fusion.7
  52.9 0.2 broadcast.15.clone
  53.1 4.6 scatter_fusion
  57.7 1.7 copy.31
  59.4 2.8 copy.32
  62.2 0.7 gather_fusion.1
  63.0 0.1 copy-done.10
  63.1 36.5 %all_gather.31 = bf16[27,16384]{1,0:T(8,128)(2,1)S(1)} all-gather(bf16[27,2048]{1,0:T(8,128)(2,1)S(1)} %copy-done.10), channel_id=1, replica_groups=mesh['fsdp'=8,'tp'=4] {'fsdp'}, dimensions={1}, use_global_device_ids=true | all-gather | bytes 995328 | tf_op jit(solution)/shard_map/all_gather | solution.py:58
  99.6 0.2 copy.45
  99.8 1.7 fusion.5
  101.5 0.2 broadcast.15.clone.1
  101.7 4.6 scatter_fusion.1
  106.3 1.7 copy.34
  107.9 2.8 copy.35
  110.7 2.0 convolution_convert_fusion.1
  112.8 5.8 %all_gather.25 = bf16[128,1024]{1,0:T(8,128)(2,1)S(1)} all-gather(bf16[128,256]{1,0:T(8,128)(2,1)S(1)} %convolution_convert_fusion.1), channel_id=1, replica_groups=mesh['fsdp'=8,'tp'=4] {'tp'}, dimensions={1}, use_global_device_ids=true | all-gather | bytes 327680 | tf_op jit(solution)/shard_map/all_gather | solution.py:53
  118.6 3.8 all-gather.9.cloned.1.call-done
  122.4 2.0 convolution_convert_fusion
  124.4 6.0 %all_gather.29 = bf16[128,1024]{1,0:T(8,128)(2,1)S(1)} all-gather(bf16[128,256]{1,0:T(8,128)(2,1)S(1)} %convolution_convert_fusion), channel_id=1, replica_groups=mesh['fsdp'=8,'tp'=4] {'tp'}, dimensions={1}, use_global_device_ids=true | all-gather | bytes 327680 | tf_op jit(solution)/shard_map/all_gather | solution.py:54
  130.4 104.2 %all-gather.7.cloned.1.call-done = bf16[1024,3584]{1,0:T(8,128)(2,1)} async-done(((bf16[128,3584]{1,0:T(8,128)(2,1)}), bf16[1024,3584]{1,0:T(8,128)(2,1)}) %all-gather.7.cloned.1.call-update) | async-done | bytes 7340048 | tf_op jit(solution)/shard_map/all_gather | solution.py:62
  234.6 5.5 %convolution_add_fusion.1 = f32[128,3584]{1,0:T(8,128)} fusion(f32[128,3584]{1,0:T(8,128)S(1)} %copy-done.7, bf16[128,1024]{1,0:T(8,128)(2,1)S(1)} %all_gather.25, bf16[1024,3584]{1,0:T(8,128)(2,1)} %all-gather.7.cloned.1.call-done), kind=kOutput, calls=%fused_computation.7 | convolution fusion | flops 939982848 | bytes 11272192 | tf_op jit(solution)/shard_map/dot_general | solution.py:72
  240.1 106.3 %all-gather.11.cloned.1.call-done = bf16[1024,3584]{1,0:T(8,128)(2,1)} async-done(((bf16[128,3584]{1,0:T(8,128)(2,1)}), bf16[1024,3584]{1,0:T(8,128)(2,1)}) %all-gather.11.cloned.1.call-update) | async-done | bytes 7340048 | tf_op jit(solution)/shard_map/all_gather | solution.py:63
  346.4 7.5 %fusion.2 = (bf16[128,3584]{1,0:T(8,128)(2,1)}, bf16[128,3584]{1,0:T(8,128)(2,1)}, bf16[128,3584]{1,0:T(8,128)(2,1)S(1)}) fusion(bf16[128,3584]{1,0:T(8,128)(2,1)} %param.23, f32[128,3584]{1,0:T(8,128)} %convolution_add_fusion.1, f32[128,3584]{1,0:T(8,128)} %copy.35, bf16[128,1024]{1,0:T(8,128)(2,1)S(1)} %all_gather.29, ...), kind=kOutput, calls=%fused_computation.12 | convolution fusion | flops 947322880 | bytes 14942208 | tf_op jit(solution)/shard_map/dot_general | solution.py:73
  353.9 1.3 copy.39
  355.1 1.7 copy.40
  356.8 0.7 gather_fusion.3
  357.5 0.5 fusion.9
  358.0 0.2 pad.5
  358.2 2.5 copy.47
  360.8 0.0 reduce-scatter.3.cloned.1.call-start
  360.9 1.1 copy-done.8
  361.9 1.3 copy.36
  363.2 1.7 copy.37
  364.9 0.7 gather_fusion.2
  365.6 0.5 fusion.11
  366.1 0.2 pad.4
  366.3 2.5 copy.46
  368.9 59.1 %reduce-scatter.5.cloned.1.call-done = f32[27,2048]{1,0:T(8,128)} async-done(((f32[27,16384]{1,0:T(8,128)}), f32[27,2048]{1,0:T(8,128)}) %reduce-scatter.5.cloned.1.call-update) | async-done | bytes 221200 | tf_op jit(solution)/shard_map/reduce_scatter | solution.py:85
  428.0 71.9 %reduce-scatter.3.cloned.1.call-done = f32[27,2048]{1,0:T(8,128)} async-done(((f32[27,16384]{1,0:T(8,128)}), f32[27,2048]{1,0:T(8,128)}) %reduce-scatter.3.cloned.1.call-update) | async-done | bytes 221200 | tf_op jit(solution)/shard_map/reduce_scatter | solution.py:84
  (43 shorter events, 0.3 us)
Async XLA Ops:
  7.2 2.9 copy-start
  7.2 103.6 %all-gather.5.cloned.1.call-start = ((), (), s32[]{:S(2)}) async-start(), calls=%async_computation.2 | async-start | bytes 2359296 | tf_op jit(solution)/shard_map/all_gather | solution.py:47
  7.9 114.5 %all-gather.9.cloned.1.call-start = ((), (), s32[]{:S(2)}) async-start(), calls=%async_computation.4 | async-start | bytes 2359296 | tf_op jit(solution)/shard_map/all_gather | solution.py:48
  8.7 226.0 %all-gather.7.cloned.1.call-start = ((), (), s32[]{:S(2)}) async-start(), calls=%async_computation.3 | async-start | bytes 8257536 | tf_op jit(solution)/shard_map/all_gather | solution.py:62
  9.4 337.0 %all-gather.11.cloned.1.call-start = ((), (), s32[]{:S(2)}) async-start(), calls=%async_computation.5 | async-start | bytes 8257536 | tf_op jit(solution)/shard_map/all_gather | solution.py:63
  10.0 418.0 %reduce-scatter.5.cloned.1.call-start = ((), (), s32[]{:S(2)}) async-start(), calls=%async_computation.7 | async-start | bytes 2359296 | tf_op jit(solution)/shard_map/reduce_scatter | solution.py:85
  10.0 1.4 copy-start.9
  11.4 38.4 %copy-start.1 = (bf16[128,32,128]{2,0,1:T(8,128)(2,1)}, bf16[128,32,128]{2,0,1:T(8,128)(2,1)S(1)}, u32[]{:S(2)}) copy-start(bf16[128,32,128]{2,0,1:T(8,128)(2,1)S(1)} %copy.30) | copy-start | bytes 3145732
  11.4 37.6 %copy-start.13 = (s32[27]{0:T(128)S(1)}, s32[27]{0:T(128)}, u32[]{:S(2)}) copy-start(s32[27]{0:T(128)} %param.16) | copy-start | bytes 328
  47.8 2.0 copy-start.11
  47.8 2.0 copy-start.12
  49.8 3.1 copy-start.3
  59.4 2.8 copy-start.14
  59.4 2.9 copy-start.2
  62.2 0.9 copy-start.10
  63.1 38.4 %copy-start.5 = (bf16[27,128,128]{2,1,0:T(8,128)(2,1)}, bf16[27,128,128]{2,1,0:T(8,128)(2,1)S(1)}, u32[]{:S(2)}) copy-start(bf16[27,128,128]{2,1,0:T(8,128)(2,1)S(1)} %gather_fusion.1) | copy-start | bytes 2654212
  118.6 116.1 %copy-start.7 = (f32[128,3584]{1,0:T(8,128)S(1)}, f32[128,3584]{1,0:T(8,128)}, u32[]{:S(2)}) copy-start(f32[128,3584]{1,0:T(8,128)} %copy.32) | copy-start | bytes 5505028
  355.1 2.4 copy-start.6
  360.8 1.2 copy-start.8
  360.8 139.1 %reduce-scatter.3.cloned.1.call-start = ((), (), s32[]{:S(2)}) async-start(), calls=%async_computation.6 | async-start | bytes 2359296 | tf_op jit(solution)/shard_map/reduce_scatter | solution.py:84
  363.2 2.4 copy-start.4
Sparse Core Ops, SparseCore 0:
  10.1 57.4 all-gather.4
  69.7 52.5 all-gather.8
  124.6 110.0 all-gather.6
  236.7 109.6 all-gather.10
  360.9 67.0 reduce-scatter.4
  431.9 67.9 reduce-scatter.2
where the time goes:
time: 507 us
  waiting for transfers between devices  348 us (69%)
  blocking collectives  84.6 us (17%)
  local copies, waits for them, and re-layouts  27.7 us (5%)
  matrix products  22.7 us (4%)
  between operations  14.4 us (3%)
  other arithmetic  9.16 us (2%)
    all_gather x1, waiting for transfers between devices, on_device(): right_up = lax.all_gather(up_right, 'fsdp', axis=0, tiled=True)  106 us
    all_gather x1, waiting for transfers between devices, on_device(): right_gate = lax.all_gather(gate_right, 'fsdp', axis=0, tiled=True)  104 us
    reduce_scatter x1, waiting for transfers between devices, on_device(): lax.psum_scatter(value_gate, 'fsdp', scatter_dimension=1, tiled=True)  71.9 us
    reduce_scatter x1, waiting for transfers between devices, on_device(): lax.psum_scatter(value_up, 'fsdp', scatter_dimension=1, tiled=True)  59.1 us
    all_gather x1, blocking collectives, on_device(): lax.all_gather(up_values, 'fsdp', axis=1, tiled=True)  36.5 us
    all_gather x1, blocking collectives, on_device(): lax.all_gather(gate_values, 'fsdp', axis=1, tiled=True)  36.4 us
  transfers between devices with their start and end apart: 6, of which 5 were waited for; matrix products, arithmetic and copies ran while one was open for 9% of the time, Pallas kernels for 0%

commit v1 on v0

--- a/solution.py
+++ b/solution.py
@@ -4,6 +4,17 @@
 from jax.sharding import PartitionSpec as P
 
 BLK = 128
+
+
+def gather_by_hops(x, mesh_axis, dim):
+    count = lax.axis_size(mesh_axis)
+    right = [(i, (i + 1) % count) for i in range(count)]
+    parts = [x]
+    for far in range(1, count):
+        parts = [lax.ppermute(parts[0], mesh_axis, right), *parts]
+    whole = jnp.concatenate(parts, axis=dim)
+    places = (lax.axis_index(mesh_axis) + 1) * parts[-1].shape[dim]
+    return jnp.roll(whole, places, axis=dim)
 
 
 def support_forward(tokens, blocks, rows, cols_local, col_blocks):
@@ -59,7 +70,7 @@
     )
     blocks_gate = flat_gate.reshape(flat_gate.shape[0], BLK, BLK)
     blocks_up = flat_up.reshape(flat_up.shape[0], BLK, BLK)
-    right_gate = lax.all_gather(gate_right, "fsdp", axis=0, tiled=True)
+    right_gate = gather_by_hops(gate_right, "fsdp", 0)
     right_up = lax.all_gather(up_right, "fsdp", axis=0, tiled=True)
     col_blocks = right_gate.shape[1] // BLK
     col_base = lax.axis_index("tp") * col_blocks

time: 507 us -> 528 us (1.041)
  waiting for transfers between devices: 348 us -> 280 us
  blocking collectives: 84.6 us -> 145 us
  local copies, waits for them, and re-layouts: 27.7 us -> 55.3 us
    ppermute x0 -> x7, waiting for transfers between devices: none -> 144 us  [gather_by_hops(): parts = [lax.ppermute(parts[0], mesh_axis, right), *parts]]
    all_gather x1, waiting for transfers between devices: 106 us -> 0.01 us  [on_device(): right_up = lax.all_gather(up_right, 'fsdp', axis=0, tiled=True)]
    all_gather x1 -> x0, waiting for transfers between devices: 104 us -> none  [on_device(): right_gate = lax.all_gather(gate_right, 'fsdp', axis=0, tiled=True)]
    all_gather x1, blocking collectives: 36.5 us -> 67.1 us  [on_device(): lax.all_gather(up_values, 'fsdp', axis=1, tiled=True)]
    all_gather x1, blocking collectives: 36.4 us -> 66.1 us  [on_device(): lax.all_gather(gate_values, 'fsdp', axis=1, tiled=True)]
    unnamed x37 -> x68, local copies, waits for them, and re-layouts: 8.89 us -> 34.5 us
  transfers between devices with their start and end apart: 6 -> 12, of which waited for: 5 -> 7; matrix products, arithmetic and copies ran while one was open for 9% -> 12% of each run, Pallas kernels for 0% -> 0%
where the time goes in v1:
time: 528 us; the launch traced here: 527 us
  waiting for transfers between devices  280 us (53%)
  blocking collectives  145 us (27%)
  local copies, waits for them, and re-layouts  55.3 us (10%)
  matrix products  20.3 us (4%)
  between operations  14.1 us (3%)
  other arithmetic  9.16 us (2%)
    ppermute x7, waiting for transfers between devices, gather_by_hops(): parts = [lax.ppermute(parts[0], mesh_axis, right), *parts]  144 us
    reduce_scatter x1, waiting for transfers between devices, on_device(): lax.psum_scatter(value_gate, 'fsdp', scatter_dimension=1, tiled=True)  71.8 us
    all_gather x1, blocking collectives, on_device(): lax.all_gather(up_values, 'fsdp', axis=1, tiled=True)  67.1 us
    all_gather x1, blocking collectives, on_device(): lax.all_gather(gate_values, 'fsdp', axis=1, tiled=True)  66.1 us
    reduce_scatter x1, waiting for transfers between devices, on_device(): lax.psum_scatter(value_up, 'fsdp', scatter_dimension=1, tiled=True)  62 us
    unnamed x68, local copies, waits for them, and re-layouts  34.5 us
  transfers between devices with their start and end apart: 12, of which 7 were waited for; matrix products, arithmetic and copies ran while one was open for 12% of the time, Pallas kernels for 0%

profile of v1, /device:TPU:0, one launch (start us, length us, event | category | flops | bytes accessed | tf_op | source)
XLA Modules:
  0.0 527.1 jit_solution(484226704910111339)
XLA Ops:
  8.7 3.0 collective-permute-start
  11.7 32.0 %collective-permute-done = bf16[128,3584]{1,0:T(8,128)(2,1)S(1)} collective-permute-done((bf16[128,3584]{1,0:T(8,128)(2,1)}, bf16[128,3584]{1,0:T(8,128)(2,1)S(1)}, u32[]{:S(2)}, u32[]{:S(2)}) %collective-permute-start) | collective-permute-done | bytes 917536 | tf_op jit(solution)/shard_map/ppermute | solution.py:14
  43.8 40.3 %collective-permute-done.1 = bf16[128,3584]{1,0:T(8,128)(2,1)S(1)} collective-permute-done((bf16[128,3584]{1,0:T(8,128)(2,1)S(1)}, bf16[128,3584]{1,0:T(8,128)(2,1)S(1)}, u32[]{:S(2)}, u32[]{:S(2)}) %collective-permute-start.1) | collective-permute-done | bytes 917536 | tf_op jit(solution)/shard_map/ppermute | solution.py:14
  84.2 31.9 %collective-permute-done.2 = bf16[128,3584]{1,0:T(8,128)(2,1)S(1)} collective-permute-done((bf16[128,3584]{1,0:T(8,128)(2,1)S(1)}, bf16[128,3584]{1,0:T(8,128)(2,1)S(1)}, u32[]{:S(2)}, u32[]{:S(2)}) %collective-permute-start.2) | collective-permute-done | bytes 917536 | tf_op jit(solution)/shard_map/ppermute | solution.py:14
  117.0 39.9 %collective-permute-done.3 = bf16[128,3584]{1,0:T(8,128)(2,1)} collective-permute-done((bf16[128,3584]{1,0:T(8,128)(2,1)S(1)}, bf16[128,3584]{1,0:T(8,128)(2,1)}, u32[]{:S(2)}, u32[]{:S(2)}) %collective-permute-start.3) | collective-permute-done | bytes 917536 | tf_op jit(solution)/shard_map/ppermute | solution.py:14
  156.9 67.1 %all_gather.27 = bf16[27,16384]{1,0:T(8,128)(2,1)} all-gather(bf16[27,2048]{1,0:T(8,128)(2,1)} %param.20), channel_id=1, replica_groups=mesh['fsdp'=8,'tp'=4] {'fsdp'}, dimensions={1}, use_global_device_ids=true | all-gather | bytes 995328 | tf_op jit(solution)/shard_map/all_gather | solution.py:69
  224.0 1.3 copy.29
  225.3 1.7 copy.30
  227.1 2.9 copy.45
  230.8 3.1 fusion.10
  234.1 4.6 scatter_fusion.1
  238.7 1.7 copy.34
  240.4 2.8 copy.35
  244.0 66.1 %all_gather.23 = bf16[27,16384]{1,0:T(8,128)(2,1)S(1)} all-gather(bf16[27,2048]{1,0:T(8,128)(2,1)S(1)} %copy-done.17), channel_id=1, replica_groups=mesh['fsdp'=8,'tp'=4] {'fsdp'}, dimensions={1}, use_global_device_ids=true | all-gather | bytes 995328 | tf_op jit(solution)/shard_map/all_gather | solution.py:68
  310.4 1.6 fusion.12
  312.3 4.6 scatter_fusion
  316.8 1.7 copy.31
  318.6 2.8 copy.32
  321.4 2.0 convolution_convert_fusion
  323.4 5.9 %all_gather.25 = bf16[128,1024]{1,0:T(8,128)(2,1)S(1)} all-gather(bf16[128,256]{1,0:T(8,128)(2,1)S(1)} %convolution_convert_fusion), channel_id=1, replica_groups=mesh['fsdp'=8,'tp'=4] {'tp'}, dimensions={1}, use_global_device_ids=true | all-gather | bytes 327680 | tf_op jit(solution)/shard_map/all_gather | solution.py:65
  329.3 2.0 convolution_convert_fusion.1
  331.4 6.0 %all_gather.22 = bf16[128,1024]{1,0:T(8,128)(2,1)S(1)} all-gather(bf16[128,256]{1,0:T(8,128)(2,1)S(1)} %convolution_convert_fusion.1), channel_id=1, replica_groups=mesh['fsdp'=8,'tp'=4] {'tp'}, dimensions={1}, use_global_device_ids=true | all-gather | bytes 327680 | tf_op jit(solution)/shard_map/all_gather | solution.py:64
  337.6 1.0 constant_dynamic-update-slice_fusion.15
  338.6 2.2 constant_dynamic-update-slice_fusion.14
  340.8 2.2 constant_dynamic-update-slice_fusion.13
  343.1 2.3 constant_dynamic-update-slice_fusion.12
  346.3 1.0 constant_dynamic-update-slice_fusion.10
  347.4 1.0 constant_dynamic-update-slice_fusion.9
  348.4 1.0 constant_dynamic-update-slice_fusion.8
  349.4 1.1 constant_dynamic-update-slice_fusion.7
  350.5 2.3 constant_dynamic-update-slice_fusion.6
  352.7 2.1 constant_dynamic-update-slice_fusion.5
  354.9 2.2 constant_dynamic-update-slice_fusion.4
  357.0 1.0 constant_dynamic-update-slice_fusion.3
  358.0 1.0 constant_dynamic-update-slice_fusion.2
  359.1 1.0 constant_dynamic-update-slice_fusion.1
  360.1 1.0 constant_dynamic-update-slice_fusion
  361.1 4.4 convolution_add_fusion
  365.5 6.2 %fusion.7 = (bf16[128,3584]{1,0:T(8,128)(2,1)}, bf16[128,3584]{1,0:T(8,128)(2,1)}, bf16[128,3584]{1,0:T(8,128)(2,1)S(1)}) fusion(f32[128,3584]{1,0:T(8,128)S(1)} %convolution_add_fusion, bf16[128,3584]{1,0:T(8,128)(2,1)S(1)} %copy-done.20, f32[128,3584]{1,0:T(8,128)S(1)} %copy-done.15, bf16[128,1024]{1,0:T(8,128)(2,1)S(1)} %all_gather.22, ...), kind=kOutput, calls=%fused_computation.14 | convolution fusion | flops 947322880 | bytes 14942212 | tf_op jit(solution)/shard_map/dot_general | solution.py:83
  371.7 1.3 copy.39
  373.0 1.7 copy.40
  376.1 2.6 copy.47
  378.7 1.1 copy-done.16
  379.8 1.3 copy.36
  381.1 1.7 copy.37
  384.2 2.5 copy.46
  386.7 62.0 %reduce-scatter.5.cloned.1.call-done = f32[27,2048]{1,0:T(8,128)} async-done(((f32[27,16384]{1,0:T(8,128)}), f32[27,2048]{1,0:T(8,128)}) %reduce-scatter.5.cloned.1.call-update) | async-done | bytes 221200 | tf_op jit(solution)/shard_map/reduce_scatter | solution.py:96
  448.7 71.8 %reduce-scatter.3.cloned.1.call-done = f32[27,2048]{1,0:T(8,128)} async-done(((f32[27,16384]{1,0:T(8,128)}), f32[27,2048]{1,0:T(8,128)}) %reduce-scatter.3.cloned.1.call-update) | async-done | bytes 221200 | tf_op jit(solution)/shard_map/reduce_scatter | solution.py:95
  (86 shorter events, 8.8 us)
Async XLA Ops:
  7.2 216.9 %copy-start = (bf16[128,4096]{1,0:T(8,128)(2,1)S(1)}, bf16[128,4096]{1,0:T(8,128)(2,1)}, u32[]{:S(2)}) copy-start(bf16[128,4096]{1,0:T(8,128)(2,1)} %param.12) | copy-start | bytes 3145732
  7.2 314.2 %all-gather.6.cloned.1.call-start = ((), (), s32[]{:S(2)}) async-start(), calls=%async_computation.3 | async-start | bytes 2359296 | tf_op jit(solution)/shard_map/all_gather | solution.py:59
  7.9 321.4 %all-gather.4.cloned.1.call-start = ((), (), s32[]{:S(2)}) async-start(), calls=%async_computation.2 | async-start | bytes 2359296 | tf_op jit(solution)/shard_map/all_gather | solution.py:58
  8.7 352.4 %all-gather.8.cloned.1.call-start = ((), (), s32[]{:S(2)}) async-start(), calls=%async_computation.4 | async-start | bytes 8257536 | tf_op jit(solution)/shard_map/all_gather | solution.py:74
  8.7 35.1 %collective-permute-start = (bf16[128,3584]{1,0:T(8,128)(2,1)}, bf16[128,3584]{1,0:T(8,128)(2,1)S(1)}, u32[]{:S(2)}, u32[]{:S(2)}) collective-permute-start(bf16[128,3584]{1,0:T(8,128)(2,1)} %param.14), channel_id=1, source_target_pairs={{0,4},{4,8},{8,12},{12,16},{16,20},{20,24},{24,28},{28,0},{1,5},{5... | collective-permute-start | bytes 2752520 | tf_op jit(solution)/shard_map/ppermute | solution.py:14
  43.8 181.6 %copy-start.9 = (bf16[128,3584]{1,0:T(8,128)(2,1)}, bf16[128,3584]{1,0:T(8,128)(2,1)S(1)}, u32[]{:S(2)}) copy-start(bf16[128,3584]{1,0:T(8,128)(2,1)S(1)} %collective-permute-done) | copy-start | bytes 2752516
  43.8 40.4 %collective-permute-start.1 = (bf16[128,3584]{1,0:T(8,128)(2,1)S(1)}, bf16[128,3584]{1,0:T(8,128)(2,1)S(1)}, u32[]{:S(2)}, u32[]{:S(2)}) collective-permute-start(bf16[128,3584]{1,0:T(8,128)(2,1)S(1)} %collective-permute-done), channel_id=1, source_target_pairs={{0,4},{4,8},{8,12},{12,16},{16,20},{20,24},{24,28},{28,0},{1,5},{5... | collective-permute-start | bytes 2752520 | tf_op jit(solution)/shard_map/ppermute | solution.py:14
  43.8 404.9 %reduce-scatter.5.cloned.1.call-start = ((), (), s32[]{:S(2)}) async-start(), calls=%async_computation.6 | async-start | bytes 2359296 | tf_op jit(solution)/shard_map/reduce_scatter | solution.py:96
  84.2 141.1 %copy-start.11 = (bf16[128,3584]{1,0:T(8,128)(2,1)}, bf16[128,3584]{1,0:T(8,128)(2,1)S(1)}, u32[]{:S(2)}) copy-start(bf16[128,3584]{1,0:T(8,128)(2,1)S(1)} %collective-permute-done.1) | copy-start | bytes 2752516
  84.2 31.9 %collective-permute-start.2 = (bf16[128,3584]{1,0:T(8,128)(2,1)S(1)}, bf16[128,3584]{1,0:T(8,128)(2,1)S(1)}, u32[]{:S(2)}, u32[]{:S(2)}) collective-permute-start(bf16[128,3584]{1,0:T(8,128)(2,1)S(1)} %collective-permute-done.1), channel_id=1, source_target_pairs={{0,4},{4,8},{8,12},{12,16},{16,20},{20,24},{24,28},{28,0},{1,5},{5... | collective-permute-start | bytes 2752520 | tf_op jit(solution)/shard_map/ppermute | solution.py:14
  116.1 0.9 copy-start.13
  117.0 39.9 %collective-permute-start.3 = (bf16[128,3584]{1,0:T(8,128)(2,1)S(1)}, bf16[128,3584]{1,0:T(8,128)(2,1)}, u32[]{:S(2)}, u32[]{:S(2)}) collective-permute-start(bf16[128,3584]{1,0:T(8,128)(2,1)S(1)} %collective-permute-done.2), channel_id=1, source_target_pairs={{0,4},{4,8},{8,12},{12,16},{16,20},{20,24},{24,28},{28,0},{1,5},{5... | collective-permute-start | bytes 2752520 | tf_op jit(solution)/shard_map/ppermute | solution.py:14
  156.9 77.0 %collective-permute-start.4 = (bf16[128,3584]{1,0:T(8,128)(2,1)}, bf16[128,3584]{1,0:T(8,128)(2,1)}, u32[]{:S(2)}, u32[]{:S(2)}) collective-permute-start(bf16[128,3584]{1,0:T(8,128)(2,1)} %collective-permute-done.3), channel_id=1, source_target_pairs={{0,4},{4,8},{8,12},{12,16},{16,20},{20,24},{24,28},{28,0},{1,5},{5... | collective-permute-start | bytes 2752520 | tf_op jit(solution)/shard_map/ppermute | solution.py:14
  225.3 4.6 copy-start.21
  227.0 3.7 copy-start.1
  227.0 3.7 copy-start.18
  227.0 3.7 copy-start.19
  230.7 3.2 copy-start.3
  230.7 3.2 copy-start.22
  233.9 87.4 %collective-permute-start.5 = (bf16[128,3584]{1,0:T(8,128)(2,1)}, bf16[128,3584]{1,0:T(8,128)(2,1)}, u32[]{:S(2)}, u32[]{:S(2)}) collective-permute-start(bf16[128,3584]{1,0:T(8,128)(2,1)} %collective-permute-done.4), channel_id=1, source_target_pairs={{0,4},{4,8},{8,12},{12,16},{16,20},{20,24},{24,28},{28,0},{1,5},{5... | collective-permute-start | bytes 2752520 | tf_op jit(solution)/shard_map/ppermute | solution.py:14
  240.4 2.9 copy-start.2
  240.4 3.6 copy-start.17
  244.0 68.0 %copy-start.5 = (bf16[27,128,128]{2,1,0:T(8,128)(2,1)}, bf16[27,128,128]{2,1,0:T(8,128)(2,1)S(1)}, u32[]{:S(2)}) copy-start(bf16[27,128,128]{2,1,0:T(8,128)(2,1)S(1)} %gather_fusion) | copy-start | bytes 2654212
  321.3 16.3 %collective-permute-start.6 = (bf16[128,3584]{1,0:T(8,128)(2,1)}, bf16[128,3584]{1,0:T(8,128)(2,1)S(1)}, u32[]{:S(2)}, u32[]{:S(2)}) collective-permute-start(bf16[128,3584]{1,0:T(8,128)(2,1)} %collective-permute-done.5), channel_id=1, source_target_pairs={{0,4},{4,8},{8,12},{12,16},{16,20},{20,24},{24,28},{28,0},{1,5},{5... | collective-permute-start | bytes 2752520 | tf_op jit(solution)/shard_map/ppermute | solution.py:14
  340.8 4.5 copy-start.14
  343.1 3.3 copy-start.12
  345.3 2.0 copy-start.10
  346.3 2.0 copy-start.8
  359.1 2.0 copy-start.7
  361.1 4.4 copy-start.15
  361.1 4.4 copy-start.20
  373.0 2.4 copy-start.4
  378.6 1.2 copy-start.16
  378.7 141.9 %reduce-scatter.3.cloned.1.call-start = ((), (), s32[]{:S(2)}) async-start(), calls=%async_computation.5 | async-start | bytes 2359296 | tf_op jit(solution)/shard_map/reduce_scatter | solution.py:95
  381.1 2.4 copy-start.6
Sparse Core Ops, SparseCore 0:
  10.1 70.4 all-gather.5
  82.7 70.8 all-gather.3
  155.8 165.0 all-gather.7
  378.8 69.9 reduce-scatter.4
  452.7 67.7 reduce-scatter.2
